TPU v7x, 32 devices: a whole 2x2x4 slice. The times are simulated.
32 devices in a mesh: dp: 8 (over y, x, core), tensor: 4 (over z).
Axes of the slice: x: 2, y: 2, z: 4, core: 2. Of those that a mesh axis runs over, the one named last changes fastest.
Arguments:
- tokens: bfloat16 [16384, 768], P('dp'), may hold values from -6 to 6
- w_qkv: bfloat16 [3, 768, 768], P(None, None, 'tensor'), may hold values from -0.21875 to 0.21875
- b_qv: float32 [2, 768], P(None, 'tensor'), may hold values from -3 to 3
- w_out: bfloat16 [768, 768], P('tensor'), may hold values from -1.25 to 1.25
- b_out: float32 [768], replicated, may hold values from -3 to 3
- ln1_gain: float32 [768], replicated, may hold values from 0.25 to 1.75
- ln1_bias: float32 [768], replicated, may hold values from -3 to 3
- w_up: bfloat16 [768, 3072], P(None, 'tensor'), may hold values from -0.21875 to 0.21875
- b_up: float32 [3072], P('tensor'), may hold values from -3 to 3
- w_down: bfloat16 [3072, 768], P('tensor'), may hold values from -0.109375 to 0.109375
- b_down: float32 [768], replicated, may hold values from -3 to 3
- ln2_gain: float32 [768], replicated, may hold values from 0.25 to 1.75
- ln2_bias: float32 [768], replicated, may hold values from -3 to 3
- lengths: int32 [32], P('dp'), may hold values from 128 to 512, as said below
- picks: int32 [32, 128], P('dp'), may hold values from 0 to 512, as said below
- cotangent: float32 [16384, 768], P('dp'), may hold values from -6 to 6
Outputs:
- output: bfloat16 [16384, 768], P('dp')
- grad_tokens: float32 [16384, 768], P('dp')
- grad_w_qkv: float32 [3, 768, 768], P(None, None, 'tensor')
- grad_b_qv: float32 [2, 768], P(None, 'tensor')
- grad_w_out: float32 [768, 768], P('tensor')
- grad_b_out: float32 [768], replicated
- grad_ln1_gain: float32 [768], replicated
- grad_ln1_bias: float32 [768], replicated
- grad_w_up: float32 [768, 3072], P(None, 'tensor')
- grad_b_up: float32 [3072], P('tensor')
- grad_w_down: float32 [3072, 768], P('tensor')
- grad_b_down: float32 [768], replicated
- grad_ln2_gain: float32 [768], replicated
- grad_ln2_bias: float32 [768], replicated
Inputs may be any that keep to these rules, and one draw needn't show every extreme that they name: `lengths`: some sequences have the full length 512. `picks`: each row lists distinct positions of its sequence in its first slots and the value 512 in the rest; every row lists at least 16 positions and leaves at least one slot unused.
All inputs are finite; a program needn't handle non-finite values.
Results may differ from a plain program's by a relative error of at most 0.013.
The roundings to bfloat16 on the way count: a program that leaves them out, or rounds other values in their place, can miss the bound.
Values sent between devices are 32-bit elements; how exact they have to be, the bound alone decides.
A program may use at most 128 MiB of HBM per device.

v0:
```python
import jax
import jax.numpy as jnp
from jax import lax
from jax.sharding import PartitionSpec as P

HD = 64
SEQ = 512


EPS = 1e-05
SCALE = 0.125


def layer_norm(tok_rows, ln_gain, ln_shift):
    centered = tok_rows - jnp.mean(tok_rows, axis=-1, keepdims=True)
    variance = jnp.mean(centered * centered, axis=-1, keepdims=True)
    return centered * lax.rsqrt(variance + EPS) * ln_gain + ln_shift


def gelu_exact(hidden_vals):
    return jax.nn.gelu(hidden_vals, approximate=False)


def key_scores(queries, key_rows, seq_length):
    scores = (
        jnp.einsum("qhd,khd->hqk", queries, key_rows, preferred_element_type=jnp.float32) * SCALE
    )
    is_valid = jnp.arange(key_rows.shape[0]) < seq_length
    return jnp.where(is_valid[None, None, :], scores, -1e30)


def attend_forward(pieces):
    queries, key_rows, values, seq_length = pieces
    scores = key_scores(queries, key_rows, seq_length)
    row_max = jnp.max(scores, axis=-1, keepdims=True)
    exponent = jnp.exp(scores - row_max)
    row_total = jnp.sum(exponent, axis=-1, keepdims=True)
    weights = (exponent / row_total).astype(jnp.bfloat16)
    attended = jnp.einsum("hqk,khd->qhd", weights, values, preferred_element_type=jnp.float32)
    return (attended.astype(jnp.bfloat16), row_max + jnp.log(row_total))


def attend_backward(pieces):
    queries, key_rows, values, grad_attended, logsum, seq_length = pieces
    weights = jnp.exp(key_scores(queries, key_rows, seq_length) - logsum)
    grad_values = jnp.einsum(
        "hqk,qhd->khd",
        weights.astype(jnp.bfloat16),
        grad_attended,
        preferred_element_type=jnp.float32,
    )
    grad_weights = jnp.einsum(
        "qhd,khd->hqk", grad_attended, values, preferred_element_type=jnp.float32
    )
    grad_scores = weights * (grad_weights - jnp.sum(grad_weights * weights, axis=-1, keepdims=True))
    grad_scores = (grad_scores * SCALE).astype(jnp.bfloat16)
    grad_queries = jnp.einsum(
        "hqk,khd->qhd", grad_scores, key_rows, preferred_element_type=jnp.float32
    )
    grad_keys = jnp.einsum("hqk,qhd->khd", grad_scores, queries, preferred_element_type=jnp.float32)
    return (
        grad_queries.astype(jnp.bfloat16),
        grad_keys.astype(jnp.bfloat16),
        grad_values.astype(jnp.bfloat16),
    )


def body(
    tokens,
    w_qkv,
    b_qv,
    w_out,
    b_out,
    ln1_gain,
    ln1_bias,
    w_up,
    b_up,
    w_down,
    b_down,
    ln2_gain,
    ln2_bias,
    lengths,
    picks,
    cotangent,
):
    tok_rows = tokens.shape[0]
    seq_count = lengths.shape[0]
    head_width = w_qkv.shape[2]
    head_count = head_width // HD

    def split_heads(flat_rows):
        return flat_rows.reshape(seq_count, SEQ, head_count, HD)

    projected = jnp.einsum("td,kdc->ktc", tokens, w_qkv, preferred_element_type=jnp.float32)
    queries = (projected[0] + b_qv[0]).astype(jnp.bfloat16)
    key_rows = projected[1].astype(jnp.bfloat16)
    values = (projected[2] + b_qv[1]).astype(jnp.bfloat16)
    attended, logsum = lax.map(
        attend_forward, (split_heads(queries), split_heads(key_rows), split_heads(values), lengths)
    )
    attended_flat = attended.reshape(tok_rows, head_width)
    attn_total = lax.psum(
        jnp.dot(attended_flat, w_out, preferred_element_type=jnp.float32), "tensor"
    )
    first_sum = tokens.astype(jnp.float32) + attn_total + b_out
    normed, pull_first = jax.vjp(layer_norm, first_sum, ln1_gain, ln1_bias)
    normed_low = normed.astype(jnp.bfloat16)
    ffn_inner = jnp.dot(normed_low, w_up, preferred_element_type=jnp.float32) + b_up
    active, pull_gelu = jax.vjp(gelu_exact, ffn_inner)
    active_low = active.astype(jnp.bfloat16)
    ffn_total = lax.psum(jnp.dot(active_low, w_down, preferred_element_type=jnp.float32), "tensor")
    second_sum = normed + ffn_total + b_down
    output, pull_second = jax.vjp(layer_norm, second_sum, ln2_gain, ln2_bias)
    positions = jnp.arange(SEQ)
    keep_mask = jnp.any(picks[:, :, None] == positions[None, None, :], axis=1)
    grad_output = cotangent * keep_mask.reshape(tok_rows, 1).astype(jnp.float32)
    grad_second, grad_ln2_gain, grad_ln2_bias = pull_second(grad_output)
    grad_b_down = jnp.sum(grad_second, axis=0)
    second_low = grad_second.astype(jnp.bfloat16)
    grad_w_down = jnp.dot(active_low.T, second_low, preferred_element_type=jnp.float32)
    grad_active = jnp.dot(second_low, w_down.T, preferred_element_type=jnp.float32)
    grad_inner = pull_gelu(grad_active)[0].astype(jnp.bfloat16)
    grad_b_up = jnp.sum(grad_inner, axis=0, dtype=jnp.float32)
    grad_w_up = jnp.dot(normed_low.T, grad_inner, preferred_element_type=jnp.float32)
    ffn_back = lax.psum(jnp.dot(grad_inner, w_up.T, preferred_element_type=jnp.float32), "tensor")
    grad_normed = grad_second + ffn_back
    grad_first, grad_ln1_gain, grad_ln1_bias = pull_first(grad_normed)
    grad_b_out = jnp.sum(grad_first, axis=0)
    first_low = grad_first.astype(jnp.bfloat16)
    grad_w_out = jnp.dot(attended_flat.T, first_low, preferred_element_type=jnp.float32)
    grad_attended = jnp.dot(first_low, w_out.T, preferred_element_type=jnp.float32).astype(
        jnp.bfloat16
    )
    grad_queries, grad_keys, grad_values = lax.map(
        attend_backward,
        (
            split_heads(queries),
            split_heads(key_rows),
            split_heads(values),
            split_heads(grad_attended),
            logsum,
            lengths,
        ),
    )
    grad_proj = jnp.stack(
        [
            grad_queries.reshape(tok_rows, head_width),
            grad_keys.reshape(tok_rows, head_width),
            grad_values.reshape(tok_rows, head_width),
        ]
    )
    grad_w_qkv = jnp.einsum("td,ktc->kdc", tokens, grad_proj, preferred_element_type=jnp.float32)
    grad_b_qv = jnp.stack(
        [
            jnp.sum(grad_proj[0], axis=0, dtype=jnp.float32),
            jnp.sum(grad_proj[2], axis=0, dtype=jnp.float32),
        ]
    )
    input_back = lax.psum(
        jnp.einsum("ktc,kdc->td", grad_proj, w_qkv, preferred_element_type=jnp.float32), "tensor"
    )
    grad_tokens = grad_first + input_back
    summed = lax.psum(
        (
            grad_w_qkv,
            grad_b_qv,
            grad_w_out,
            grad_b_out,
            grad_ln1_gain,
            grad_ln1_bias,
            grad_w_up,
            grad_b_up,
            grad_w_down,
            grad_b_down,
            grad_ln2_gain,
            grad_ln2_bias,
        ),
        "dp",
    )
    (
        grad_w_qkv,
        grad_b_qv,
        grad_w_out,
        grad_b_out,
        grad_ln1_gain,
        grad_ln1_bias,
        grad_w_up,
        grad_b_up,
        grad_w_down,
        grad_b_down,
        grad_ln2_gain,
        grad_ln2_bias,
    ) = summed
    return (
        output.astype(jnp.bfloat16),
        grad_tokens,
        grad_w_qkv,
        grad_b_qv,
        grad_w_out,
        grad_b_out,
        grad_ln1_gain,
        grad_ln1_bias,
        grad_w_up,
        grad_b_up,
        grad_w_down,
        grad_b_down,
        grad_ln2_gain,
        grad_ln2_bias,
    )


def solution(mesh):
    in_specs = (
        P("dp", None),
        P(None, None, "tensor"),
        P(None, "tensor"),
        P("tensor", None),
        P(),
        P(),
        P(),
        P(None, "tensor"),
        P("tensor"),
        P("tensor", None),
        P(),
        P(),
        P(),
        P("dp"),
        P("dp", None),
        P("dp", None),
    )
    out_specs = (
        P("dp", None),
        P("dp", None),
        P(None, None, "tensor"),
        P(None, "tensor"),
        P("tensor", None),
        P(),
        P(),
        P(),
        P(None, "tensor"),
        P("tensor"),
        P("tensor", None),
        P(),
        P(),
        P(),
    )
    return jax.shard_map(body, mesh=mesh, in_specs=in_specs, out_specs=out_specs, check_vma=False)
```

profile of v0, /device:TPU:0, one launch (start us, length us, event | category | flops | bytes accessed | tf_op | source)
XLA Modules:
  0.0 1285.4 jit_solution(4883626915768980597)
XLA Ops:
  25.8 24.7 %while.26 = (s32[]{:T(128)}, bf16[4,512,3,64]{1,3,2,0:T(8,128)(2,1)S(1)}, f32[4,3,512,1]{2,1,3,0:T(4,128)}, bf16[4,512,3,64]{1,3,2,0:T(8,128)(2,1)}, s32[4]{0:T(...) while((s32[]{:T(128)}, ...), condition=%wide.region_3.4_spmd, body=%wide.region_0.3_spmd.sunk | while | flops 210861056 | bytes 10283621 | solution.py:98
  57.1 225.5 %all-reduce.8.cloned.1.call-done = f32[2048,768]{1,0:T(8,128)} async-done(((f32[2048,768]{1,0:T(8,128)}), f32[2048,768]{1,0:T(8,128)}) %all-reduce.8.cloned.1.call-update) | async-done | bytes 6291472 | tf_op jit(solution)/shard_map/psum | solution.py:102
  289.9 18.3 %multiply_convert_fusion.1 = (bf16[2048,768]{1,0:T(8,128)(2,1)S(1)}, f32[2048,768]{1,0:T(8,128)}, f32[2048,768]{1,0:T(8,128)}) fusion(f32[768]{0:T(1024)S(1)} %copy-done.28, bf16[2048,768]{1,0:T(8,128)(2,1)S(1)} %fusion.88, bf16[768,768]{1,0:T(8,128)(2,1)S(1)} %copy-done), kind=kOutput, calls=%fused_computation.81 | convolution fusion | flops 2519728128 | bytes 20057088 | tf_op jit(solution)/shard_map/dot_general | solution.py:108
  315.4 221.0 %all-reduce.10.cloned.1.call-done = f32[2048,768]{1,0:T(8,128)} async-done(((f32[2048,768]{1,0:T(8,128)}), f32[2048,768]{1,0:T(8,128)}) %all-reduce.10.cloned.1.call-update) | async-done | bytes 6291472 | tf_op jit(solution)/shard_map/psum | solution.py:111
  543.0 5.8 multiply_reduce_fusion.1
  553.5 9.6 convert_reduce_fusion
  569.7 221.5 %all-reduce.12.cloned.1.call-done = f32[2048,768]{1,0:T(8,128)} async-done(((f32[2048,768]{1,0:T(8,128)}), f32[2048,768]{1,0:T(8,128)}) %all-reduce.12.cloned.1.call-update) | async-done | bytes 6291472 | tf_op jit(solution)/shard_map/psum | solution.py:125
  791.2 8.7 multiply_reduce_fusion.2
  810.1 98.3 %while.27 = (s32[]{:T(128)}, bf16[4,512,3,64]{1,3,2,0:T(8,128)(2,1)S(1)}, bf16[4,512,3,64]{1,3,2,0:T(8,128)(2,1)}, bf16[4,512,3,64]{1,3,2,0:T(8,128)(2,1)S(1)}, ...) while((s32[]{:T(128)}, ...), condition=%wide.region_18.19_spmd, body=%wide.region_16.18_spmd.sunk | while | flops 514626048 | bytes 36593792 | solution.py:134
  819.6 6.7 fusion.165
  826.2 6.0 fusion.164
  844.1 6.6 fusion.165
  850.8 6.0 fusion.164
  868.7 6.6 fusion.165
  875.4 6.0 fusion.164
  893.3 6.6 fusion.165
  899.9 6.0 fusion.164
  925.2 7.2 convolution_bitcast_fusion
  932.4 7.1 fusion.112
  939.5 7.1 fusion.100
  953.3 200.9 %all-reduce.14.cloned.1.call-done = f32[2048,768]{1,0:T(8,128)} async-done(((f32[2048,768]{1,0:T(8,128)}), f32[2048,768]{1,0:T(8,128)}) %all-reduce.14.cloned.1.call-update) | async-done | bytes 6291472 | tf_op jit(solution)/shard_map/psum | solution.py:159
  1154.2 7.7 add_reduce_fusion
  1161.9 26.2 %all-reduce = (f32[2,192]{1,0:T(2,128)}, f32[768]{0:T(1024)}, f32[768]{0:T(1024)}, f32[768]{0:T(1024)}, f32[768]{0:T(1024)}, /*index=5*/f32[768]{0:T(1024)}, f32[768]{0:T(1024)}, f32[768]{0:T(1024)}) all-reduce(f32[2,192]{1,0:T(2,128)S(1)} %pad_maximum_fusion, ...), channel_id=1, replica_groups=mesh['dp'=8,'tensor'=4] {'dp'}, use_global_device_ids=true, to_apply=%region_23.24 | all-reduce | flops 5760 | bytes 46080 | tf_op jit(solution)/shard_map/psum | solution.py:163
  1188.2 82.9 %all-reduce.16.cloned.1.call-done = (f32[3,768,192]{1,2,0:T(8,128)}, f32[192,768]{1,0:T(8,128)}, f32[768,768]{1,0:T(8,128)}, f32[768,768]{1,0:T(8,128)}) async-done(((f32[3,768,192]{1,2,0:T(8,128)}, f32[192,768]{1,0:T(8,128)}, f32[768,768]{1,0:T(8,128)}, f32[768,768]{1,0:T(8,128)}), (f32[3,768,192]{1,2,0:T(8,128)}, f32[192,768]{1,0:T(8,128)}, f32[768,768]{1,0:T(8,128)}, ...) | async-done | bytes 7077904 | tf_op jit(solution)/shard_map/psum | solution.py:163
  (201 shorter events, 170.8 us)
Async XLA Ops:
  7.2 282.7 %copy-start = (bf16[768,768]{1,0:T(8,128)(2,1)S(1)}, bf16[768,768]{1,0:T(8,128)(2,1)}, u32[]{:S(2)}) copy-start(bf16[768,768]{1,0:T(8,128)(2,1)} %param.27) | copy-start | bytes 3538948
  7.2 275.4 %all-reduce.8.cloned.1.call-start = ((), (), s32[]{:S(2)}) async-start(), calls=%async_computation | async-start | bytes 12582912 | tf_op jit(solution)/shard_map/psum | solution.py:102
  11.5 7.7 copy-start.25
  16.0 9.7 copy-start.29
  52.2 230.5 %copy-start.23 = (f32[768]{0:T(1024)S(1)}, f32[768]{0:T(1024)}, u32[]{:S(2)}) copy-start(f32[768]{0:T(1024)} %param.24) | copy-start | bytes 9220
  56.9 479.5 %all-reduce.10.cloned.1.call-start = ((), (), s32[]{:S(2)}) async-start(), calls=%async_computation.1 | async-start | bytes 12582912 | tf_op jit(solution)/shard_map/psum | solution.py:111
  289.9 18.3 %copy-start.7 = (bf16[2048,768]{1,0:T(8,128)(2,1)}, bf16[2048,768]{1,0:T(8,128)(2,1)S(1)}, u32[]{:S(2)}) copy-start(bf16[2048,768]{1,0:T(8,128)(2,1)S(1)} %fusion.88) | copy-start | bytes 9437188
  289.9 20.1 %copy-start.27 = (bf16[768,768]{1,0:T(8,128)(2,1)S(1)}, bf16[768,768]{1,0:T(8,128)(2,1)}, u32[]{:S(2)}) copy-start(bf16[768,768]{1,0:T(8,128)(2,1)} %param.29) | copy-start | bytes 3538948
  314.4 221.9 %copy-start.24 = (f32[768]{0:T(1024)S(1)}, f32[768]{0:T(1024)}, u32[]{:S(2)}) copy-start(f32[768]{0:T(1024)} %param.30) | copy-start | bytes 9220
  314.5 476.7 %all-reduce.12.cloned.1.call-start = ((), (), s32[]{:S(2)}) async-start(), calls=%async_computation.2 | async-start | bytes 12582912 | tf_op jit(solution)/shard_map/psum | solution.py:125
  543.0 10.4 slice-start.4
  553.5 9.6 copy-start.3
  569.3 585.0 %all-reduce.14.cloned.1.call-start = ((), (), s32[]{:S(2)}) async-start(), calls=%async_computation.3 | async-start | bytes 12582912 | tf_op jit(solution)/shard_map/psum | solution.py:159
  932.3 338.7 %all-reduce.16.cloned.1.call-start = ((), (), s32[]{:S(2)}) async-start(), calls=%async_computation.4 | async-start | bytes 14155776 | tf_op jit(solution)/shard_map/psum | solution.py:163
  932.4 7.1 copy-start.32
  932.4 14.2 %slice-start = ((s8[6291456]{0:T(1024)(128)(4,1)}), s8[4194304]{0:T(1024)(128)(4,1)S(1)}, s32[]{:S(2)}) async-start(s8[6291456]{0:T(1024)(128)(4,1)} %bitcast.150), calls=%async_computation.5 | async-start | bytes 8388608
  939.5 7.1 slice-start.1
  939.5 7.1 copy-start.5
  953.3 208.6 %copy-start.15 = (f32[768]{0:T(1024)S(1)}, f32[768]{0:T(1024)}, u32[]{:S(2)}) copy-start(f32[768]{0:T(1024)} %get-tuple-element.162) | copy-start | bytes 9220
  953.3 208.6 %copy-start.16 = (f32[768]{0:T(1024)S(1)}, f32[768]{0:T(1024)}, u32[]{:S(2)}) copy-start(f32[768]{0:T(1024)} %get-tuple-element.166) | copy-start | bytes 9220
  953.3 208.6 %copy-start.18 = (f32[768]{0:T(1024)S(1)}, f32[768]{0:T(1024)}, u32[]{:S(2)}) copy-start(f32[768]{0:T(1024)} %get-tuple-element.164) | copy-start | bytes 9220
  953.3 208.6 %copy-start.19 = (f32[768]{0:T(1024)S(1)}, f32[768]{0:T(1024)}, u32[]{:S(2)}) copy-start(f32[768]{0:T(1024)} %get-tuple-element.167) | copy-start | bytes 9220
  953.3 208.6 %copy-start.20 = (f32[768]{0:T(1024)S(1)}, f32[768]{0:T(1024)}, u32[]{:S(2)}) copy-start(f32[768]{0:T(1024)} %get-tuple-element.230) | copy-start | bytes 9220
  953.3 208.6 %copy-start.22 = (f32[768]{0:T(1024)S(1)}, f32[768]{0:T(1024)}, u32[]{:S(2)}) copy-start(f32[768]{0:T(1024)} %get-tuple-element.236) | copy-start | bytes 9220
  (20 other events, 67.2 us)
Sparse Core Ops, SparseCore 0:
  57.0 225.5 all-reduce.7
  314.6 221.7 all-reduce.9
  569.4 221.7 all-reduce.11
  932.5 221.7 all-reduce.13
  1158.9 112.0 all-reduce.15
where the time goes:
time: 1290 us
  waiting for transfers between devices  952 us (74%)
  matrix products  176 us (14%)
  other arithmetic  58.9 us (5%)
  local copies, waits for them, and re-layouts  57.2 us (4%)
  blocking collectives  26.2 us (2%)
  between operations  14.6 us (1%)
    psum x1, waiting for transfers between devices, body(): lax.psum(jnp.dot(attended_flat, w_out, preferred_element_type=jnp.float32...  226 us
    psum x1, waiting for transfers between devices, body(): lax.psum(jnp.dot(grad_inner, w_up.T, preferred_element_type=jnp.float32),...  221 us
    psum x1, waiting for transfers between devices, body(): lax.psum(jnp.dot(active_low, w_down, preferred_element_type=jnp.float32),...  221 us
    psum x1, waiting for transfers between devices, body(): lax.psum(jnp.einsum('ktc,kdc->td', grad_proj, w_qkv, preferred_element_ty...  201 us
    psum x1, waiting for transfers between devices, body(): lax.psum((grad_w_qkv, grad_b_qv, grad_w_out, grad_b_out, grad_ln1_gain, g...  82.9 us
    dot_general x4, matrix products, attend_backward(): jnp.einsum('hqk,qhd->khd', grad_scores, queries, preferred_element_type=j...  26.5 us
    psum x1, blocking collectives, body(): lax.psum((grad_w_qkv, grad_b_qv, grad_w_out, grad_b_out, grad_ln1_gain, g...  26.2 us
  transfers between devices with their start and end apart: 5, of which 5 were waited for; matrix products, arithmetic and copies ran while one was open for 2% of the time, Pallas kernels for 0%

commit v1 on v0

v1 whole, which is shorter than its diff:
```python
import functools

import jax
import jax.numpy as jnp
from jax import lax
from jax.experimental import pallas as pl
from jax.experimental.pallas import tpu as pltpu
from jax.sharding import PartitionSpec as P

HD = 64
PAIR = 2 * HD
EPS = 1e-05
SCALE = 0.125
NEG = -1e30
F32 = jnp.float32
BF16 = jnp.bfloat16


def dot(a, b, ca, cb):
    return lax.dot_general(a, b, (((ca,), (cb,)), ((), ())), preferred_element_type=F32)


def halves(block):
    lane = lax.broadcasted_iota(jnp.int32, block.shape, 1)
    zero = jnp.zeros_like(block)
    return jnp.concatenate([jnp.where(lane < HD, block, zero), jnp.where(lane < HD, zero, block)], axis=0)


def merge(stacked):
    rows = stacked.shape[0] // 2
    lane = lax.broadcasted_iota(jnp.int32, (rows, PAIR), 1)
    return jnp.where(lane < HD, stacked[:rows], stacked[rows:])


def softmax_rows(stacked_q, keys, length):
    scores = dot(stacked_q * SCALE, keys, 1, 1)
    key_at = lax.broadcasted_iota(jnp.int32, (1, keys.shape[0]), 1)
    scores = scores + jnp.where(key_at < length, 0.0, NEG)
    top = jnp.max(scores, axis=-1, keepdims=True)
    e = jnp.exp(scores - top)
    return e / jnp.sum(e, axis=-1, keepdims=True)


def attend_kernel(first_ref, lengths_ref, q_ref, k_ref, v_ref, o_ref):
    length = lengths_ref[first_ref[0] + pl.program_id(0)]
    p = softmax_rows(halves(q_ref[0]), k_ref[0], length)
    o_ref[0] = merge(dot(p.astype(BF16), v_ref[0], 1, 0)).astype(BF16)


def attend(first, lengths, q, k, v):
    n, rows, width = q.shape
    keys = k.shape[1]
    return pl.pallas_call(
        attend_kernel,
        grid_spec=pltpu.PrefetchScalarGridSpec(
            num_scalar_prefetch=2,
            grid=(n, width // PAIR),
            in_specs=[
                pl.BlockSpec((1, rows, PAIR), lambda s, h, f, l: (s, 0, h)),
                pl.BlockSpec((1, keys, PAIR), lambda s, h, f, l: (f[0] + s, 0, h)),
                pl.BlockSpec((1, keys, PAIR), lambda s, h, f, l: (f[0] + s, 0, h)),
            ],
            out_specs=pl.BlockSpec((1, rows, PAIR), lambda s, h, f, l: (s, 0, h)),
        ),
        out_shape=jax.ShapeDtypeStruct(q.shape, BF16),
        cost_estimate=pl.CostEstimate(
            flops=4 * n * rows * keys * width * 4, bytes_accessed=4 * n * (rows + keys) * width,
            transcendentals=n * rows * keys * width // HD,
        ),
        name="attend",
    )(first, lengths, q, k, v)


def attend_back_kernel(lengths_ref, q_ref, k_ref, v_ref, g_ref, dq_ref, dk_ref, dv_ref):
    length = lengths_ref[pl.program_id(0)]
    q = halves(q_ref[0])
    g = halves(g_ref[0])
    k = k_ref[0]
    p = softmax_rows(q, k, length)
    dv_ref[0] = dot(p.astype(BF16), g, 0, 0).astype(BF16)
    dp = dot(g, v_ref[0], 1, 1)
    ds = p * (dp - jnp.sum(dp * p, axis=-1, keepdims=True))
    ds = (ds * SCALE).astype(BF16)
    dq_ref[0] = merge(dot(ds, k, 1, 0)).astype(BF16)
    dk_ref[0] = dot(ds, q, 0, 0).astype(BF16)


def attend_back(lengths, q, k, v, g):
    n, rows, width = q.shape
    keys = k.shape[1]
    q_spec = pl.BlockSpec((1, rows, PAIR), lambda s, h, l: (s, 0, h))
    k_spec = pl.BlockSpec((1, keys, PAIR), lambda s, h, l: (s, 0, h))
    return pl.pallas_call(
        attend_back_kernel,
        grid_spec=pltpu.PrefetchScalarGridSpec(
            num_scalar_prefetch=1,
            grid=(n, width // PAIR),
            in_specs=[q_spec, k_spec, k_spec, q_spec],
            out_specs=[q_spec, k_spec, k_spec],
        ),
        out_shape=[
            jax.ShapeDtypeStruct(q.shape, BF16),
            jax.ShapeDtypeStruct(k.shape, BF16),
            jax.ShapeDtypeStruct(k.shape, BF16),
        ],
        cost_estimate=pl.CostEstimate(
            flops=10 * n * rows * keys * width * 4, bytes_accessed=4 * n * (rows + 2 * keys) * width,
            transcendentals=n * rows * keys * width // HD,
        ),
        name="attend_back",
    )(lengths, q, k, v, g)


def norm_parts(y):
    centered = y - jnp.mean(y, axis=-1, keepdims=True)
    rstd = lax.rsqrt(jnp.mean(centered * centered, axis=-1, keepdims=True) + EPS)
    return centered * rstd, rstd


def norm_back(grad, gain, hat, rstd):
    scaled = grad * gain
    return rstd * (
        scaled
        - jnp.mean(scaled, axis=-1, keepdims=True)
        - hat * jnp.mean(scaled * hat, axis=-1, keepdims=True)
    )


def mm(a, b):
    return jnp.dot(a, b, preferred_element_type=F32)


def mm_nt(a, b):
    return lax.dot_general(a, b, (((1,), (1,)), ((), ())), preferred_element_type=F32)


def mm_tn(a, b):
    return lax.dot_general(a, b, (((0,), (0,)), ((), ())), preferred_element_type=F32)


def gather_rows(one, ranks, copies, which, *parts):
    shares = [p.reshape(copies, p.shape[0] // copies, p.shape[1]) for p in parts]
    mine = jnp.concatenate(
        [lax.dynamic_index_in_dim(s, which, 0, keepdims=False) for s in shares], axis=0
    ).astype(F32)
    whole = lax.all_gather(mine, ("tensor", "dp"), tiled=False) * one
    whole = whole.reshape(ranks, copies, mine.shape[0], mine.shape[1])
    out, at = [], 0
    for s in shares:
        out.append(
            whole[:, :, at : at + s.shape[1]].astype(BF16).reshape(ranks, copies * s.shape[1], s.shape[2])
        )
        at += s.shape[1]
    return out


def body(
    ranks, copies, tokens, w_qkv, b_qv, w_out, b_out, ln1_gain, ln1_bias, w_up, b_up, w_down, b_down,
    ln2_gain, ln2_bias, lengths, picks, cotangent,
):
    rank = lax.axis_index("tensor")
    which = lax.axis_index("dp")
    seqs = lengths.shape[0]
    rows, width = tokens.shape
    seq = rows // seqs
    slots = picks.shape[1]
    part = w_qkv.shape[2]
    hidden = w_up.shape[1]
    own = seqs // ranks

    one = jnp.where(lengths[0] > 0, 1.0, 0.0).astype(F32)

    own_qkv = jnp.swapaxes(w_qkv, 1, 2).reshape(3 * part, width)
    (all_qkv,) = gather_rows(one, ranks, copies, which, own_qkv)
    all_qkv = jnp.swapaxes(all_qkv.reshape(ranks, 3, part, width), 0, 1).reshape(3, ranks * part, width)
    all_out, all_up, all_down = gather_rows(one, ranks, copies, which, w_out, w_up, w_down)
    all_out = all_out.reshape(ranks * part, width)
    all_down = all_down.reshape(ranks * hidden, width)
    all_up = jnp.swapaxes(all_up, 0, 1).reshape(width, ranks * hidden)
    vectors = lax.all_gather(jnp.concatenate([b_qv.reshape(-1), b_up]), "tensor")
    all_b_qv = jnp.swapaxes(vectors[:, : 2 * part].reshape(ranks, 2, part), 0, 1).reshape(2, ranks * part)
    all_b_up = vectors[:, 2 * part :].reshape(-1)

    by_seq = tokens.reshape(seqs, seq, width)
    chosen = (picks[:, :, None] == jnp.arange(seq)[None, None, :])
    chosen_low = chosen.astype(BF16)
    chosen_f32 = chosen.astype(F32)
    picked = jnp.einsum("spk,skd->spd", chosen_low, by_seq, preferred_element_type=F32).astype(BF16)
    grad_output = jnp.einsum(
        "spk,skd->spd", chosen_f32, cotangent.reshape(seqs, seq, width),
        precision=lax.Precision.HIGH, preferred_element_type=F32,
    ).reshape(seqs * slots, width)
    first = rank * own
    own_tokens = lax.dynamic_slice_in_dim(tokens, first * seq, own * seq, 0)
    n_own = own * seq
    used = jnp.concatenate([own_tokens, picked.reshape(seqs * slots, width)], axis=0)

    keys = mm_nt(tokens, all_qkv[1]).astype(BF16).reshape(seqs, seq, width)
    values = (mm_nt(tokens, all_qkv[2]) + all_b_qv[1]).astype(BF16).reshape(seqs, seq, width)
    queries = (mm_nt(used, all_qkv[0]) + all_b_qv[0]).astype(BF16)
    q_picked = queries[n_own:].reshape(seqs, slots, width)
    zero = jnp.zeros((1,), jnp.int32)
    att_own = attend(first.reshape(1), lengths, queries[:n_own].reshape(own, seq, width), keys, values)
    att_picked = attend(zero, lengths, q_picked, keys, values)
    attended = jnp.concatenate([att_own.reshape(n_own, width), att_picked.reshape(-1, width)], axis=0)

    first_sum = used.astype(F32) + mm(attended, all_out) + b_out
    hat1, rstd1 = norm_parts(first_sum)
    normed = hat1 * ln1_gain + ln1_bias
    normed_low = normed.astype(BF16)
    inner = mm(normed_low, all_up) + all_b_up
    cdf = 0.5 * (1.0 + lax.erf(inner * 0.7071067811865476))
    active = (inner * cdf).astype(BF16)
    second_sum = normed + mm(active, all_down) + b_down
    hat2, rstd2 = norm_parts(second_sum)
    out_own = hat2[:n_own] * ln2_gain + ln2_bias
    output = (lax.all_gather(out_own, "tensor", tiled=True) * one).astype(BF16)

    hat2, rstd2, hat1, rstd1 = hat2[n_own:], rstd2[n_own:], hat1[n_own:], rstd1[n_own:]
    inner, cdf, active, normed_low = inner[n_own:], cdf[n_own:], active[n_own:], normed_low[n_own:]
    att = attended[n_own:]
    grad_second = norm_back(grad_output, ln2_gain, hat2, rstd2)
    g_ln2_gain = jnp.sum(grad_output * hat2, axis=0)
    g_ln2_bias = jnp.sum(grad_output, axis=0)
    g_b_down = jnp.sum(grad_second, axis=0)
    second_low = grad_second.astype(BF16)
    own_hidden = lambda x: lax.dynamic_slice_in_dim(x, rank * hidden, hidden, 1)
    own_part = lambda x: lax.dynamic_slice_in_dim(x, rank * part, part, x.ndim - 1)
    g_w_down = lax.psum(mm_tn(own_hidden(active), second_low), "dp")
    grad_active = mm_nt(second_low, all_down)
    slope = cdf + inner * (0.3989422804014327 * jnp.exp(-0.5 * inner * inner))
    grad_inner = (grad_active * slope).astype(BF16)
    own_inner = own_hidden(grad_inner)
    g_b_up = jnp.sum(own_inner, axis=0, dtype=F32)
    g_w_up = lax.psum(mm_tn(normed_low, own_inner), "dp")
    grad_normed = grad_second + mm_nt(grad_inner, all_up)
    grad_first = norm_back(grad_normed, ln1_gain, hat1, rstd1)
    g_ln1_gain = jnp.sum(grad_normed * hat1, axis=0)
    g_ln1_bias = jnp.sum(grad_normed, axis=0)
    g_b_out = jnp.sum(grad_first, axis=0)
    first_low = grad_first.astype(BF16)
    g_w_out = lax.psum(mm_tn(own_part(att), first_low), "dp")
    grad_att = mm_nt(first_low, all_out).astype(BF16)
    dq, dk, dv = attend_back(lengths, q_picked, keys, values, grad_att.reshape(seqs, slots, width))
    dq_rows = dq.reshape(seqs * slots, width)
    dk_rows = dk.reshape(rows, width)
    dv_rows = dv.reshape(rows, width)
    sparse = (grad_first + mm(dq_rows, all_qkv[0])).reshape(seqs, slots, width)
    grad_tokens = (
        jnp.einsum("spk,spd->skd", chosen_f32, sparse, precision=lax.Precision.HIGH,
                   preferred_element_type=F32).reshape(rows, width)
        + mm(dk_rows, all_qkv[1])
        + mm(dv_rows, all_qkv[2])
    )
    own_q, own_k, own_v = own_part(dq_rows), own_part(dk_rows), own_part(dv_rows)
    g_w_qkv = jnp.stack([
        mm_tn(picked.reshape(seqs * slots, width), own_q), mm_tn(tokens, own_k), mm_tn(tokens, own_v),
    ])
    g_b_qv = jnp.stack([jnp.sum(own_q, axis=0, dtype=F32), jnp.sum(own_v, axis=0, dtype=F32)])
    g_w_qkv, g_b_qv, g_b_out, g_ln1_gain, g_ln1_bias, g_b_up, g_b_down, g_ln2_gain, g_ln2_bias = lax.psum(
        (g_w_qkv, g_b_qv, g_b_out, g_ln1_gain, g_ln1_bias, g_b_up, g_b_down, g_ln2_gain, g_ln2_bias), "dp"
    )
    return (
        output, grad_tokens, g_w_qkv, g_b_qv, g_w_out, g_b_out, g_ln1_gain, g_ln1_bias, g_w_up, g_b_up,
        g_w_down, g_b_down, g_ln2_gain, g_ln2_bias,
    )


def solution(mesh):
    in_specs = (
        P("dp", None), P(None, None, "tensor"), P(None, "tensor"), P("tensor", None), P(), P(), P(),
        P(None, "tensor"), P("tensor"), P("tensor", None), P(), P(), P(), P("dp"), P("dp", None), P("dp", None),
    )
    out_specs = (
        P("dp", None), P("dp", None), P(None, None, "tensor"), P(None, "tensor"), P("tensor", None), P(), P(),
        P(), P(None, "tensor"), P("tensor"), P("tensor", None), P(), P(), P(),
    )
    step = functools.partial(body, mesh.shape["tensor"], mesh.shape["dp"])
    return jax.shard_map(step, mesh=mesh, in_specs=in_specs, out_specs=out_specs, check_vma=False)
```

time: 1290 us -> 537 us (0.42)
  waiting for transfers between devices: 952 us -> 241 us
  matrix products: 176 us -> 86.4 us
  Pallas kernels: 0 us -> 60.1 us
  other arithmetic: 58.9 us -> 30.8 us
  blocking collectives: 26.2 us -> 41.1 us
    psum x5 -> x1, waiting for transfers between devices: 952 us -> 111 us  [body(): lax.psum((g_w_qkv, g_b_qv, g_b_out, g_ln1_gain, g_ln1_bias, g_b_up, g_b_d...]
    all_gather x0 -> x3, waiting for transfers between devices: none -> 130 us  [the longest x2 124 us: gather_rows(): whole = lax.all_gather(mine, ('tensor', 'dp'), tiled=False) * one]
    dot_general x40 -> x21, matrix products: 176 us -> 86.4 us  [the longest x6 35.2 us: mm(): return jnp.dot(a, b, preferred_element_type=F32)]
    pallas_call x0 -> x3, Pallas kernels: none -> 60.1 us  [the longest x2 32.8 us: attend(): pl.pallas_call(attend_kernel, grid_spec=pltpu.PrefetchScalarGridSpec(num_...]
    reduce_sum x15 -> x8, other arithmetic: 46.2 us -> 8.28 us  [the longest x1 2.09 us: body(): g_b_down = jnp.sum(grad_second, axis=0)]
    all_gather x0 -> x1, blocking collectives: none -> 14.9 us  [body(): lax.all_gather(jnp.concatenate([b_qv.reshape(-1), b_up]), 'tensor')]
  transfers between devices with their start and end apart: 5 -> 4, of which waited for: 5 -> 4; matrix products, arithmetic and copies ran while one was open for 2% -> 19% of each run, Pallas kernels for 0% -> 11%
where the time goes in v1:
time: 537 us; the launch traced here: 527 us
  waiting for transfers between devices  241 us (45%)
  matrix products  86.4 us (16%)
  Pallas kernels  60.1 us (11%)
  local copies, waits for them, and re-layouts  51.7 us (10%)
  blocking collectives  41.1 us (8%)
  other arithmetic  30.8 us (6%)
  between operations  15.4 us (3%)
    all_gather x2, waiting for transfers between devices, gather_rows(): whole = lax.all_gather(mine, ('tensor', 'dp'), tiled=False) * one  124 us
    psum x1, waiting for transfers between devices, body(): lax.psum((g_w_qkv, g_b_qv, g_b_out, g_ln1_gain, g_ln1_bias, g_b_up, g_b_d...  111 us
    dot_general x6, matrix products, mm(): return jnp.dot(a, b, preferred_element_type=F32)  35.2 us
    pallas_call x2, Pallas kernels, attend(): pl.pallas_call(attend_kernel, grid_spec=pltpu.PrefetchScalarGridSpec(num_...  32.8 us
    pallas_call x1, Pallas kernels, attend_back(): pl.pallas_call(attend_back_kernel, grid_spec=pltpu.PrefetchScalarGridSpec...  27.3 us
    dot_general x6, matrix products, mm_nt(): lax.dot_general(a, b, (((1,), (1,)), ((), ())), preferred_element_type=F32)  26.4 us
    psum x1, blocking collectives, body(): lax.psum((g_w_qkv, g_b_qv, g_b_out, g_ln1_gain, g_ln1_bias, g_b_up, g_b_d...  26.1 us
    dot_general x6, matrix products, mm_tn(): lax.dot_general(a, b, (((0,), (0,)), ((), ())), preferred_element_type=F32)  15.9 us
  transfers between devices with their start and end apart: 4, of which 4 were waited for; matrix products, arithmetic and copies ran while one was open for 19% of the time, Pallas kernels for 11%

profile of v1, /device:TPU:0, one launch (start us, length us, event | category | flops | bytes accessed | tf_op | source)
XLA Modules:
  0.0 526.5 jit_solution(5568303170675818510)
XLA Ops:
  13.3 14.9 %all-gather.1 = f32[4,1,1152]{2,1,0:T(1,128)S(1)} all-gather(f32[1,1,1152]{2,1,0:T(1,128)S(1)} %reshape.275), channel_id=2, replica_groups=mesh['dp'=8,'tensor'=4] {'tensor'}, dimensions={0}, use_global_device_ids=true | all-gather | bytes 23040 | tf_op jit(solution)/shard_map/all_gather | solution.py:180
  30.2 5.5 %fusion.42 = (f32[768]{0:T(1024)S(1)}, f32[4,128]{1,0:T(4,128)S(1)}, f32[4,128,768]{2,1,0:T(8,128)}) fusion(f32[768]{0:T(1024)S(1)} %copy-done.20, f32[4,512,768]{2,1,0:T(8,128)} %bitcast.107, s32[4,128]{1,0:T(4,128)S(1)} %copy-done.21), kind=kOutput, calls=%fused_computation.103 | convolution fusion | flops 1209400064 | bytes 7874560 | tf_op jit(solution)/shard_map/spk,skd->spd/dot_general | solution.py:189
  37.3 49.1 %all-gather.6.cloned.1.call-done = f32[32,72,768]{2,1,0:T(8,128)} async-done(((f32[1,72,768]{2,1,0:T(8,128)}), f32[32,72,768]{2,1,0:T(8,128)}) %all-gather.6.cloned.1.call-update) | async-done | bytes 7077904 | tf_op jit(solution)/shard_map/all_gather | solution.py:146
  92.6 4.2 fusion.8
  96.8 4.7 copy.45
  101.5 5.3 fusion.7
  106.7 4.7 copy.44
  115.9 21.4 %attend.3 = bf16[4,128,768]{2,1,0:T(8,128)(2,1)} custom-call(s32[1]{0:T(128)} %constant.55.clone.1.first_ref, s32[4]{0:T(128)} %lengths_ref.5, bf16[4,128,768]{2,1,0:T(8,128)(2,1)} %bitcast.137, bf16[4,512,768]{2,1,0:T(8,128)(2,1)} %bitcast.127, bf16[4,512,768]{2,1,0:T(8,128)(2,1)} %bitcast.124), custom_call_target="tpu_custom_call" | custom-call | flops 3221225472 | bytes 7864320 | tf_op jit(solution)/shard_map/attend/pallas_call | solution.py:53
  137.3 11.5 %attend.2 = bf16[1,512,768]{2,1,0:T(8,128)(2,1)} custom-call(s32[1]{0:T(128)} %bitcast.2.first_ref, s32[4]{0:T(128)} %lengths_ref.5, bf16[1,512,768]{2,1,0:T(8,128)(2,1)} %get-tuple-element.56.q_ref, bf16[4,512,768]{2,1,0:T(8,128)(2,1)} %bitcast.128, bf16[4,512,768]{2,1,0:T(8,128)(2,1)} %bitcast.125), custom_call_target="tpu_custom_call" | custom-call | flops 3221225472 | bytes 3145728 | tf_op jit(solution)/shard_map/attend/pallas_call | solution.py:53
  148.7 74.9 %all-gather.8.cloned.1.call-done = f32[32,216,768]{2,1,0:T(8,128)} async-done(((f32[1,216,768]{2,1,0:T(8,128)}), f32[32,216,768]{2,1,0:T(8,128)}) %all-gather.8.cloned.1.call-update) | async-done | bytes 21233680 | tf_op jit(solution)/shard_map/all_gather | solution.py:146
  223.7 8.4 %multiply_convert_fusion = bf16[32,216,768]{2,1,0:T(8,128)(2,1)S(1)} fusion(f32[32,216,768]{2,1,0:T(8,128)} %all-gather.8.cloned.1.call-done, f32[]{:T(128)} %bitcast.5), kind=kLoop, calls=%fused_computation | loop fusion | flops 10616832 | bytes 31850500 | tf_op jit(solution)/shard_map/convert.2
  232.1 4.0 copy-done.1
  237.2 8.1 %fusion.45 = (bf16[4,8,96,768]{3,2,1,0:T(8,128)(2,1)}, bf16[4,8,96,768]{3,2,1,0:T(8,128)(2,1)}) fusion(bf16[4,8,216,768]{3,2,1,0:T(8,128)(2,1)} %bitcast.101), kind=kLoop, calls=%fused_computation.106 | loop fusion | bytes 18874368 | tf_op jit(solution)/shard_map/slice | solution.py:151
  245.3 6.7 %copy.46 = bf16[768,4,768]{0,2,1:T(8,128)(2,1)} copy(bf16[768,4,768]{2,0,1:T(8,128)(2,1)} %bitcast.102) | data formatting | bytes 9437184 | tf_op jit(solution)/shard_map/transpose | solution.py:179
  258.4 11.9 %multiply_convert_fusion.1 = (bf16[1024,3072]{1,0:T(8,128)(2,1)}, f32[1024,3072]{1,0:T(8,128)}, f32[1024,3072]{1,0:T(8,128)}) fusion(f32[3072]{0:T(1024)S(1)} %add.176, bf16[1024,768]{1,0:T(8,128)(2,1)S(1)} %get-tuple-element.48, bf16[768,3072]{0,1:T(8,128)(2,1)S(1)} %bitcast.115), kind=kOutput, calls=%fused_computation.1 | convolution fusion | flops 4850712576 | bytes 37761024 | tf_op jit(solution)/shard_map/dot_general | solution.py:130
  270.4 8.9 %fusion.48 = (f32[1024]{0:T(1024)S(1)}, f32[1024,768]{1,0:T(8,128)S(1)}) fusion(f32[768]{0:T(1024)S(1)} %copy-done.26, bf16[1024,3072]{1,0:T(8,128)(2,1)} %get-tuple-element.46, bf16[3072,768]{1,0:T(8,128)(2,1)} %bitcast.119, f32[768]{0:T(1024)S(1)} %copy-done.23, f32[1024,768]{1,0:T(8,128)S(1)} %get-tuple-element.49, f32[768]{0:T(1024)S(1)} %copy-done.22), kind=kOutput, calls=%fused_computation.109 | convolution fusion | flops 4835769344 | bytes 17314816 | tf_op jit(solution)/shard_map/dot_general | solution.py:130
  283.8 3.9 slice.119
  287.7 9.1 %fusion.5 = bf16[512,3072]{1,0:T(8,128)(2,1)S(1)} fusion(f32[1024,3072]{1,0:T(8,128)} %get-tuple-element.60, f32[1024,3072]{1,0:T(8,128)} %get-tuple-element.47, bf16[3072,768]{1,0:T(8,128)(2,1)} %bitcast.120, f32[512,768]{1,0:T(8,128)S(1)} %copy-done.8), kind=kOutput, calls=%fused_computation.10 | convolution fusion | flops 2427322368 | bytes 22020096 | tf_op jit(solution)/shard_map/dot_general | solution.py:134
  303.2 27.3 %attend_back.1 = (bf16[4,128,768]{2,1,0:T(8,128)(2,1)}, bf16[4,512,768]{2,1,0:T(8,128)(2,1)}, bf16[4,512,768]{2,1,0:T(8,128)(2,1)}) custom-call(s32[4]{0:T(128)} %lengths_ref.5, bf16[4,128,768]{2,1,0:T(8,128)(2,1)} %bitcast.138, bf16[4,512,768]{2,1,0:T(8,128)(2,1)} %bitcast.129, bf16[4,512,768]{2,1,0:T(8,128)(2,1)} %bitcast.126, bf16[4,128,768]{2,1,0:T(8,128)(2,1)} %bitcast.154), custom_call_target="tpu_custom_call" | custom-call | flops 8053063680 | bytes 14155776 | tf_op jit(solution)/shard_map/attend_back/pallas_call | solution.py:93
  352.2 26.1 %all-reduce = (f32[2,192]{1,0:T(2,128)}, f32[768]{0:T(1024)}, f32[768]{0:T(1024)}, f32[768]{0:T(1024)}, f32[768]{0:T(1024)}, /*index=5*/f32[768]{0:T(1024)}, f32[768]{0:T(1024)}, f32[768]{0:T(1024)}) all-reduce(f32[2,192]{1,0:T(2,128)S(1)} %pad_maximum_fusion.4, ...), channel_id=1, replica_groups=mesh['dp'=8,'tensor'=4] {'dp'}, use_global_device_ids=true, to_apply=%region_11.12 | all-reduce | flops 5760 | bytes 46080 | tf_op jit(solution)/shard_map/psum | solution.py:260
  386.1 5.2 fusion.6
  391.3 6.1 %all-gather.10.cloned.1.call-done = f32[2048,768]{1,0:T(8,128)} async-done(((f32[512,768]{1,0:T(8,128)}), f32[2048,768]{1,0:T(8,128)}) %all-gather.10.cloned.1.call-update) | async-done | bytes 6291472 | tf_op jit(solution)/shard_map/all_gather | solution.py:217
  397.4 4.9 multiply_convert_fusion.3
  402.3 110.6 %all-reduce.4.cloned.1.call-done = (f32[3,768,192]{1,2,0:T(8,128)}, f32[192,768]{1,0:T(8,128)}, f32[768,768]{1,0:T(8,128)}, f32[768,768]{1,0:T(8,128)}) async-done(((f32[3,768,192]{1,2,0:T(8,128)}, f32[192,768]{1,0:T(8,128)}, f32[768,768]{1,0:T(8,128)}, f32[768,768]{1,0:T(8,128)}), (f32[3,768,192]{1,2,0:T(8,128)}, f32[192,768]{1,0:T(8,128)}, f32[768,768]{1,0:T(8,128)}, ...) | async-done | bytes 7077904 | tf_op jit(solution)/shard_map/psum | solution.py:260
  (133 shorter events, 73.8 us)
Async XLA Ops:
  7.2 22.0 %copy-start = (bf16[2048,768]{1,0:T(8,128)(2,1)S(1)}, bf16[2048,768]{1,0:T(8,128)(2,1)}, u32[]{:S(2)}) copy-start(bf16[2048,768]{1,0:T(8,128)(2,1)} %param.16) | copy-start | bytes 9437188
  7.2 23.0 %copy-start.21 = (s32[4,128]{1,0:T(4,128)S(1)}, s32[4,128]{1,0:T(4,128)}, u32[]{:S(2)}) copy-start(s32[4,128]{1,0:T(4,128)} %param.30) | copy-start | bytes 6148
  7.2 22.9 %copy-start.20 = (f32[768]{0:T(1024)S(1)}, f32[768]{0:T(1024)}, u32[]{:S(2)}) copy-start(f32[768]{0:T(1024)} %param.27) | copy-start | bytes 9220
  7.2 79.1 %all-gather.6.cloned.1.call-start = ((), (), s32[]{:S(2)}) async-start(), calls=%async_computation | async-start | bytes 7299072 | tf_op jit(solution)/shard_map/all_gather | solution.py:146
  9.0 214.6 %all-gather.8.cloned.1.call-start = ((), (), s32[]{:S(2)}) async-start(), calls=%async_computation.1 | async-start | bytes 21897216 | tf_op jit(solution)/shard_map/all_gather | solution.py:146
  11.8 385.6 %all-gather.10.cloned.1.call-start = ((), (), s32[]{:S(2)}) async-start(), calls=%async_computation.2 | async-start | bytes 7864320 | tf_op jit(solution)/shard_map/all_gather | solution.py:217
  232.1 4.0 copy-start.1
  245.3 6.7 %copy-start.25 = (f32[768]{0:T(1024)S(1)}, f32[768]{0:T(1024)}, u32[]{:S(2)}) copy-start(f32[768]{0:T(1024)} %param.20) | copy-start | bytes 9220
  257.0 13.3 %copy-start.10 = (bf16[1024,768]{1,0:T(8,128)(2,1)}, bf16[1024,768]{1,0:T(8,128)(2,1)S(1)}, u32[]{:S(2)}) copy-start(bf16[1024,768]{1,0:T(8,128)(2,1)S(1)} %get-tuple-element.48) | copy-start | bytes 4718596
  257.0 13.3 %copy-start.6 = (f32[1024,768]{1,0:T(8,128)}, f32[1024,768]{1,0:T(8,128)S(1)}, u32[]{:S(2)}) copy-start(f32[1024,768]{1,0:T(8,128)S(1)} %get-tuple-element.49) | copy-start | bytes 9437188
  258.4 11.9 %copy-start.26 = (f32[768]{0:T(1024)S(1)}, f32[768]{0:T(1024)}, u32[]{:S(2)}) copy-start(f32[768]{0:T(1024)} %param.26) | copy-start | bytes 9220
  283.7 229.2 %all-reduce.4.cloned.1.call-start = ((), (), s32[]{:S(2)}) async-start(), calls=%async_computation.3 | async-start | bytes 14155776 | tf_op jit(solution)/shard_map/psum | solution.py:260
  283.8 3.9 copy-start.8
  283.8 13.0 %slice-start.2 = ((s8[4718592]{0:T(1024)(128)(4,1)}), s8[4194304]{0:T(1024)(128)(4,1)S(1)}, s32[]{:S(2)}) async-start(s8[4718592]{0:T(1024)(128)(4,1)} %bitcast.116), calls=%async_computation.6 | async-start | bytes 8388608
  287.7 9.1 %copy-start.7 = (f32[1024,768]{1,0:T(8,128)S(1)}, f32[1024,768]{1,0:T(8,128)}, u32[]{:S(2)}) copy-start(f32[1024,768]{1,0:T(8,128)} %copy-done.6) | copy-start | bytes 9437188
  287.7 9.1 %slice-start.3 = ((s8[4718592]{0:T(1024)(128)(4,1)}), s8[524288]{0:T(1024)(128)(4,1)S(1)}, s32[]{:S(2)}) async-start(s8[4718592]{0:T(1024)(128)(4,1)} %bitcast.116), calls=%async_computation.7 | async-start | bytes 1048576
  296.8 3.0 copy-start.18
  334.7 3.9 copy-start.3
  337.3 3.6 copy-start.11
  340.9 3.5 copy-start.9
  383.4 2.6 copy-start.5
  383.4 2.6 copy-start.13
  513.0 3.0 copy-start.19
  513.0 3.8 copy-start.15
  (12 other events, 18.6 us)
Sparse Core Ops, SparseCore 0:
  11.5 74.8 all-gather.5
  89.8 133.7 all-gather.7
  283.9 113.4 all-gather.9
  402.1 110.8 all-reduce.3

commit v2 on v1

v2 whole, which is shorter than its diff:
```python
import functools

import jax
import jax.numpy as jnp
from jax import lax
from jax.experimental import pallas as pl
from jax.experimental.pallas import tpu as pltpu
from jax.sharding import PartitionSpec as P

HD = 64
PAIR = 2 * HD
EPS = 1e-05
SCALE = 0.125
NEG = -1e30
F32 = jnp.float32
BF16 = jnp.bfloat16
GROUP = 8
MESH_ID = pl.DeviceIdType.MESH
VMEM = 56 * 2**20


def dot(a, b, ca, cb):
    return lax.dot_general(a, b, (((ca,), (cb,)), ((), ())), preferred_element_type=F32)


def halves(block):
    lane = lax.broadcasted_iota(jnp.int32, block.shape, 1)
    zero = jnp.zeros_like(block)
    return jnp.concatenate([jnp.where(lane < HD, block, zero), jnp.where(lane < HD, zero, block)], axis=0)


def merge(stacked):
    rows = stacked.shape[0] // 2
    lane = lax.broadcasted_iota(jnp.int32, (rows, PAIR), 1)
    return jnp.where(lane < HD, stacked[:rows], stacked[rows:])


def scores_of(stacked_q, keys, length):
    scores = dot(stacked_q * SCALE, keys, 1, 1)
    key_at = lax.broadcasted_iota(jnp.int32, (1, keys.shape[0]), 1)
    scores = scores + jnp.where(key_at < length, 0.0, NEG)
    return jnp.exp(scores - jnp.max(scores, axis=-1, keepdims=True))


def softmax_rows(stacked_q, keys, length):
    e = scores_of(stacked_q, keys, length)
    return e / jnp.sum(e, axis=-1, keepdims=True)


def attend_pair(q, k, v, length):
    e = scores_of(halves(q), k, length)
    total = jnp.sum(e, axis=-1, keepdims=True)
    return merge(dot(e.astype(BF16), v, 1, 0) / total).astype(BF16)


def flip(w, bit):
    return w + bit - 2 * bit * lax.rem(w // bit, 2)


def turn(z, k):
    b0, b1 = lax.rem(z, 2), lax.rem(z // 2, 2)
    return z + (k & 1) * (1 - 2 * b0) + (k >> 1) * (2 - 4 * b1)


def front_kernel(
    ranks, chunks, x_ref, xp_ref, mine_ref, lengths_ref, head_ref, tail_ref, vec_ref,
    k_ref, v_ref, qp_ref, a_ref, out_ref, vecs_ref, w_ref,
    heads_ref, q_ref, zs, zr, xs, xr, ys, yr, ds, dr, es, er, cs, cr, ss, sr,
):
    w, z = lax.axis_index("dp"), lax.axis_index("tensor")
    low = lax.rem(w, GROUP)
    wc, wx, wy = flip(w, 1), flip(w, 2), flip(w, 4)
    share = lambda dev: lax.rem(dev, GROUP)
    across = share(flip(wx, 4))
    zk = {k: turn(z, k) for k in range(1, ranks)}
    barrier = pltpu.get_barrier_semaphore()
    peers = [{"dp": w, "tensor": zk[k]} for k in zk] + [{"dp": d, "tensor": z} for d in (wc, wx, wy)]
    for peer in peers:
        pl.semaphore_signal(barrier, inc=1, device_id=peer, device_id_type=MESH_ID)
    pl.semaphore_wait(barrier, len(peers))

    def remote(src, dst, s, r, to_w, to_z):
        return pltpu.make_async_remote_copy(
            src_ref=src, dst_ref=dst, send_sem=s, recv_sem=r,
            device_id={"dp": to_w, "tensor": to_z}, device_id_type=MESH_ID,
        )

    items = [(k, True, 0, head_ref.shape[0]) for k in zk] + [(k, False, at, n) for at, n in chunks for k in zk]

    def land(i, rank, sh, at, n):
        return (heads_ref if items[i][1] else out_ref).at[rank, sh, pl.ds(at, n)]

    def copy(i, what):
        k, _, at, n = items[i]
        h = (n // 2 + 7) // 8 * 8
        if what == "z":
            src = head_ref if items[i][1] else tail_ref
            return remote(src.at[pl.ds(at, n)], land(i, z, low, at, n), zs.at[i], zr.at[i], w, zk[k])
        sh, at, n, s, r, to = {
            "x": (low, at, n, xs.at[i], xr.at[i], wx),
            "y": (low, at, n, ys.at[i], yr.at[i], wy),
            "d": (share(wx), at, h, ds.at[i], dr.at[i], wy),
            "e": (share(wy), at + h, n - h, es.at[i], er.at[i], wx),
            0: (low, at, n, cs.at[i, 0], cr.at[i, 0], wc),
            1: (share(wx), at, n, cs.at[i, 1], cr.at[i, 1], wc),
            2: (share(wy), at, n, cs.at[i, 2], cr.at[i, 2], wc),
            3: (across, at, n, cs.at[i, 3], cr.at[i, 3], wc),
        }[what]
        ref = land(i, zk[k], sh, at, n)
        return remote(ref, ref, s, r, to, z)

    def vector_copy(k):
        return remote(vec_ref, vecs_ref.at[z], ss.at[k - 1], sr.at[k - 1], w, zk[k])

    follows = (("z", ("x", "y", 0)), ("x", ("d", 1)), ("y", ("e", 2)), ("d", ()), ("e", (3,)))
    stages = (follows[:1], follows[1:3], follows[3:])

    def steps(first, last, t):
        for lag, stage in enumerate(stages):
            i = t + first - lag
            if first <= i < last:
                for arrived, onward in stage:
                    copy(i, arrived).wait_recv()
                    for what in onward:
                        copy(i, what).start()

    for i in range(len(items)):
        copy(i, "z").start()
        if i == ranks - 2:
            for k in zk:
                vector_copy(k).start()
    nh = ranks - 1
    for t in range(nh + 2):
        steps(0, nh, t)
    for i in range(nh):
        for j in range(4):
            copy(i, j).wait_recv()
    for k in zk:
        vector_copy(k).wait_recv()
    vecs_ref[z] = vec_ref[...]

    part = mine_ref.shape[0] // 3
    for r in range(ranks):
        block = heads_ref[r].reshape(3 * part, -1)
        for i in range(3):
            w_ref[i, r * part : (r + 1) * part] = block[i * part : (i + 1) * part].astype(BF16)
    at = pl.multiple_of(z * part, part)
    for i in range(3):
        w_ref[i, pl.ds(at, part)] = mine_ref[i * part : (i + 1) * part]
    vectors = vecs_ref[0]
    for r in range(1, ranks):
        vectors = vectors + vecs_ref[r]
    bias_q, bias_v = vectors[1:2], vectors[2:3]

    seqs, _, width = x_ref.shape
    pairs = width // PAIR
    rounds = len(items) - nh + 2
    space = seqs * pairs // rounds

    def compute(t, carry):
        for j in range(rounds):
            @pl.when(t == j * space)
            def _():
                steps(nh, len(items), j)

        s, h = t // pairs, lax.rem(t, pairs)

        @pl.when(h == 0)
        def _():
            x = x_ref[s]
            k_ref[s] = dot(x, w_ref[1], 1, 1).astype(BF16)
            v_ref[s] = (dot(x, w_ref[2], 1, 1) + bias_v).astype(BF16)
            q_ref[...] = (dot(x, w_ref[0], 1, 1) + bias_q).astype(BF16)
            qp_ref[s] = (dot(xp_ref[s], w_ref[0], 1, 1) + bias_q).astype(BF16)

        cols = pl.ds(pl.multiple_of(h * PAIR, PAIR), PAIR)
        a_ref[s, :, cols] = attend_pair(q_ref[:, cols], k_ref[s, :, cols], v_ref[s, :, cols], lengths_ref[s])
        return carry

    lax.fori_loop(0, seqs * pairs, compute, 0)
    for i in range(nh, len(items)):
        for j in range(4):
            copy(i, j).wait_recv()
    for i in range(len(items)):
        for what in ("z", "x", "y", "d", "e", 0, 1, 2, 3):
            copy(i, what).wait_send()
    for k in zk:
        vector_copy(k).wait_send()


def front(ranks, chunks, x, xp, mine, lengths, head, tail, vectors):
    seqs, seq, width = x.shape
    n = (ranks - 1) * (len(chunks) + 1)
    dma = pltpu.SemaphoreType.DMA
    vmem = pl.BlockSpec(memory_space=pltpu.VMEM)
    any_space = pl.BlockSpec(memory_space=pl.ANY)
    shape = jax.ShapeDtypeStruct
    return pl.pallas_call(
        functools.partial(front_kernel, ranks, chunks),
        out_shape=[
            shape(x.shape, BF16), shape(x.shape, BF16), shape(xp.shape, BF16), shape(x.shape, BF16),
            shape((ranks, GROUP) + tail.shape, F32), shape((ranks,) + vectors.shape, F32),
            shape((3, width, width), BF16),
        ],
        in_specs=[vmem] * 3 + [pl.BlockSpec(memory_space=pltpu.SMEM)] + [any_space] * 2 + [vmem],
        out_specs=[vmem] * 4 + [any_space, vmem, vmem],
        scratch_shapes=[
            pltpu.VMEM((ranks, GROUP) + head.shape, F32), pltpu.VMEM((seq, width), BF16),
        ] + [dma((n,))] * 10 + [dma((n, 4))] * 2 + [dma((ranks - 1,))] * 2,
        compiler_params=pltpu.CompilerParams(collective_id=1, has_side_effects=True, vmem_limit_bytes=VMEM),
        name="front",
    )(x, xp, mine, lengths, head, tail, vectors)


def attend_back_kernel(lengths_ref, q_ref, k_ref, v_ref, g_ref, dq_ref, dk_ref, dv_ref):
    length = lengths_ref[pl.program_id(0)]
    q = halves(q_ref[0])
    g = halves(g_ref[0])
    k = k_ref[0]
    p = softmax_rows(q, k, length)
    dv_ref[0] = dot(p.astype(BF16), g, 0, 0).astype(BF16)
    dp = dot(g, v_ref[0], 1, 1)
    ds = p * (dp - jnp.sum(dp * p, axis=-1, keepdims=True))
    ds = (ds * SCALE).astype(BF16)
    dq_ref[0] = merge(dot(ds, k, 1, 0)).astype(BF16)
    dk_ref[0] = dot(ds, q, 0, 0).astype(BF16)


def attend_back(lengths, q, k, v, g):
    n, rows, width = q.shape
    keys = k.shape[1]
    q_spec = pl.BlockSpec((1, rows, PAIR), lambda s, h, l: (s, 0, h))
    k_spec = pl.BlockSpec((1, keys, PAIR), lambda s, h, l: (s, 0, h))
    return pl.pallas_call(
        attend_back_kernel,
        grid_spec=pltpu.PrefetchScalarGridSpec(
            num_scalar_prefetch=1,
            grid=(n, width // PAIR),
            in_specs=[q_spec, k_spec, k_spec, q_spec],
            out_specs=[q_spec, k_spec, k_spec],
        ),
        out_shape=[
            jax.ShapeDtypeStruct(q.shape, BF16),
            jax.ShapeDtypeStruct(k.shape, BF16),
            jax.ShapeDtypeStruct(k.shape, BF16),
        ],
        cost_estimate=pl.CostEstimate(
            flops=10 * n * rows * keys * width * 4, bytes_accessed=4 * n * (rows + 2 * keys) * width,
            transcendentals=n * rows * keys * width // HD,
        ),
        name="attend_back",
    )(lengths, q, k, v, g)


def norm_parts(y):
    centered = y - jnp.mean(y, axis=-1, keepdims=True)
    rstd = lax.rsqrt(jnp.mean(centered * centered, axis=-1, keepdims=True) + EPS)
    return centered * rstd, rstd


def norm_back(grad, gain, hat, rstd):
    scaled = grad * gain
    return rstd * (
        scaled
        - jnp.mean(scaled, axis=-1, keepdims=True)
        - hat * jnp.mean(scaled * hat, axis=-1, keepdims=True)
    )


def mm(a, b):
    return jnp.dot(a, b, preferred_element_type=F32)


def mm_nt(a, b):
    return lax.dot_general(a, b, (((1,), (1,)), ((), ())), preferred_element_type=F32)


def mm_tn(a, b):
    return lax.dot_general(a, b, (((0,), (0,)), ((), ())), preferred_element_type=F32)


def reduce_kernel(chunks, n_in, *refs):
    ins, outs = refs[:n_in], refs[n_in:2 * n_in]
    acc_ref, halves_ref, quarter_ref, eighth_ref, send_sem, recv_sem = refs[2 * n_in:]
    w = lax.axis_index("dp")
    z = lax.axis_index("tensor")
    bit = {"c": lax.rem(w, 2), "x": lax.rem(w // 2, 2), "y": lax.rem(w // 4, 2)}
    peer = {"c": flip(w, 1), "x": flip(w, 2), "y": flip(w, 4)}
    barrier = pltpu.get_barrier_semaphore()
    for p in peer.values():
        pl.semaphore_signal(barrier, inc=1, device_id={"dp": p, "tensor": z}, device_id_type=MESH_ID)
    pl.semaphore_wait(barrier, 3)
    def send(c, j, axis, src, dst):
        copy = pltpu.make_async_remote_copy(src_ref=src, dst_ref=dst, send_sem=send_sem.at[c, j], recv_sem=recv_sem.at[c, j],
            device_id={"dp": peer[axis], "tensor": z}, device_id_type=MESH_ID)
        copy.start()
        return copy
    def at(ref, start, n):
        return ref.at[pl.ds(pl.multiple_of(start, 8), n)]
    def add(dst, d_at, a, a_at, b, b_at, n):
        step = 16 if n % 16 == 0 else 8
        def body(i, carry):
            o = i * step
            dst[pl.ds(pl.multiple_of(d_at + o, 8), step)] = (
                a[pl.ds(pl.multiple_of(a_at + o, 8), step)] + b[pl.ds(pl.multiple_of(b_at + o, 8), step)])
            return carry
        lax.fori_loop(0, n // step, body, 0)
    copies = {}
    h_at = 0
    base = []
    for (r, o, n) in chunks:
        base.append(h_at); h_at += n
    def stage(c, s):
        r, o, n = chunks[c]
        x, out = ins[r], outs[r]
        hb, qb, eb = base[c] // 2, base[c] // 4, base[c] // 8
        half = o + bit["c"] * (n // 2)
        other = o + (1 - bit["c"]) * (n // 2)
        q, e, f = n // 4, n // 8, n // 16
        streams = (("x", "y"), ("y", "x"))
        if s == 0:
            copies[c, 0] = send(c, 0, "c", at(x, other, n // 2), halves_ref.at[pl.ds(hb, n // 2)])
        elif s == 1:
            copies[c, 0].wait_recv()
            add(acc_ref, hb, x, half, halves_ref, hb, n // 2)
            for i, (p, _) in enumerate(streams):
                copies[c, 1 + i] = send(c, 1 + i, p, at(acc_ref, hb + i * q + (1 - bit[p]) * e, e), quarter_ref.at[pl.ds(qb + i * e, e)])
        elif s == 2:
            for i, (p, p2) in enumerate(streams):
                copies[c, 1 + i].wait_recv()
                a0 = hb + i * q + bit[p] * e
                add(acc_ref, a0, acc_ref, a0, quarter_ref, qb + i * e, e)
                copies[c, 3 + i] = send(c, 3 + i, p2, at(acc_ref, a0 + (1 - bit[p2]) * f, f), eighth_ref.at[pl.ds(eb + i * f, f)])
        elif s == 3:
            for i, (p, p2) in enumerate(streams):
                copies[c, 3 + i].wait_recv()
                a1 = i * q + bit[p] * e + bit[p2] * f
                add(out, half + a1, acc_ref, hb + a1, eighth_ref, eb + i * f, f)
                a1 = half + a1
                copies[c, 5 + i] = send(c, 5 + i, p2, at(out, a1, f), at(out, a1, f))
        elif s == 4:
            for i, (p, p2) in enumerate(streams):
                copies[c, 5 + i].wait_recv()
                a0 = half + i * q + bit[p] * e
                copies[c, 7 + i] = send(c, 7 + i, p, at(out, a0, e), at(out, a0, e))
        elif s == 5:
            for i in range(2):
                copies[c, 7 + i].wait_recv()
            copies[c, 9] = send(c, 9, "c", at(out, half, n // 2), at(out, half, n // 2))
        else:
            copies[c, 9].wait_recv()
    for t in range(len(chunks) + 6):
        for s in range(7):
            if 0 <= t - s < len(chunks):
                stage(t - s, s)
    for copy in copies.values():
        copy.wait_send()

def dp_reduce(outer, arrays, step, cid):
    chunks = []
    for r, a in enumerate(arrays):
        for o in range(0, a.shape[0], step):
            chunks.append((r, o, min(step, a.shape[0] - o)))
    total = sum(n for _, _, n in chunks)
    width = arrays[0].shape[1]
    vmem = lambda rows: pltpu.VMEM((rows, width), F32)
    dma = pltpu.SemaphoreType.DMA((len(chunks), 10))
    spec = pl.BlockSpec(memory_space=pltpu.VMEM)
    sums = pl.pallas_call(
        functools.partial(reduce_kernel, tuple(chunks), len(arrays)),
        out_shape=[jax.ShapeDtypeStruct(a.shape, F32) for a in arrays],
        in_specs=[spec] * len(arrays), out_specs=[spec] * len(arrays),
        scratch_shapes=[vmem(total // 2), vmem(total // 2), vmem(total // 4), vmem(total // 8), dma, dma],
        compiler_params=pltpu.CompilerParams(collective_id=cid, has_side_effects=True, vmem_limit_bytes=VMEM),
        name="dp_reduce",
    )(*arrays)
    if outer is not None:
        sums = [lax.psum(a, "dp", axis_index_groups=outer) for a in sums]
    return sums


def my_share(which, p):
    return lax.dynamic_index_in_dim(
        p.reshape(GROUP, p.shape[0] // GROUP, p.shape[1]), lax.rem(which, GROUP), 0, keepdims=False
    )


def body(
    ranks, outer, tokens, w_qkv, b_qv, w_out, b_out, ln1_gain, ln1_bias, w_up, b_up, w_down, b_down,
    ln2_gain, ln2_bias, lengths, picks, cotangent,
):
    rank = lax.axis_index("tensor")
    which = lax.axis_index("dp")
    seqs = lengths.shape[0]
    rows, width = tokens.shape
    seq = rows // seqs
    slots = picks.shape[1]
    part = w_qkv.shape[2]
    hidden = w_up.shape[1]

    by_seq = tokens.reshape(seqs, seq, width)
    chosen = (picks[:, :, None] == jnp.arange(seq)[None, None, :])
    chosen_low = chosen.astype(BF16)
    chosen_f32 = chosen.astype(F32)
    picked = jnp.einsum("spk,skd->spd", chosen_low, by_seq, preferred_element_type=F32).astype(BF16)
    picked_rows = picked.reshape(seqs * slots, width)

    own_qkv = jnp.swapaxes(w_qkv, 1, 2).reshape(3 * part, width)
    row_out, row_up, row_down = w_out.shape[0] // GROUP, hidden // GROUP, hidden // GROUP
    head = my_share(which, own_qkv).astype(F32)
    tail = jnp.concatenate([my_share(which, p) for p in (w_out, w_up.T, w_down)], axis=0).astype(F32)
    spots = lax.dynamic_update_slice_in_dim(jnp.zeros((2, width), F32), b_qv, rank * part, 1)
    vectors = jnp.concatenate([b_up.reshape(1, width), spots, jnp.zeros((5, width), F32)], axis=0)
    cut = row_out + row_up
    keys, values, q_picked, attended, gathered, all_vectors, all_qkv = front(
        ranks, ((0, cut), (cut, row_down)), by_seq, picked, own_qkv, lengths, head, tail, vectors
    )
    all_b_up = all_vectors[:, 0].reshape(-1)

    def whole(at, n, mine):
        block = gathered[:, :, at : at + n].astype(BF16).reshape(ranks, GROUP * n, width)
        return lax.dynamic_update_index_in_dim(block, mine, rank, 0).reshape(-1, width)

    all_out = whole(0, row_out, w_out)
    all_up = whole(row_out, row_up, w_up.T)
    all_down = whole(cut, row_down, w_down)
    att_picked = jnp.einsum("spk,skd->spd", chosen_low, attended, preferred_element_type=F32).astype(BF16)
    grad_output = jnp.einsum(
        "spk,skd->spd", chosen_f32, cotangent.reshape(seqs, seq, width),
        precision=lax.Precision.HIGH, preferred_element_type=F32,
    ).reshape(seqs * slots, width)
    def forward(tok, att):
        first_sum = tok.astype(F32) + mm(att, all_out) + b_out
        hat1, rstd1 = norm_parts(first_sum)
        normed = hat1 * ln1_gain + ln1_bias
        normed_low = normed.astype(BF16)
        inner = mm_nt(normed_low, all_up) + all_b_up
        cdf = 0.5 * (1.0 + lax.erf(inner * 0.7071067811865476))
        active = (inner * cdf).astype(BF16)
        hat2, rstd2 = norm_parts(normed + mm(active, all_down) + b_down)
        return hat1, rstd1, normed_low, inner, cdf, active, hat2, rstd2

    output = (forward(tokens, attended.reshape(rows, width))[6] * ln2_gain + ln2_bias).astype(BF16)

    att = att_picked.reshape(-1, width)
    hat1, rstd1, normed_low, inner, cdf, active, hat2, rstd2 = forward(picked_rows, att)
    grad_second = norm_back(grad_output, ln2_gain, hat2, rstd2)
    g_ln2_gain = jnp.sum(grad_output * hat2, axis=0)
    g_ln2_bias = jnp.sum(grad_output, axis=0)
    g_b_down = jnp.sum(grad_second, axis=0)
    second_low = grad_second.astype(BF16)
    own_hidden = lambda x: lax.dynamic_slice_in_dim(x, rank * hidden, hidden, 1)
    own_part = lambda x: lax.dynamic_slice_in_dim(x, rank * part, part, x.ndim - 1)
    g_w_down = mm_tn(own_hidden(active), second_low)
    grad_active = mm_nt(second_low, all_down)
    slope = cdf + inner * (0.3989422804014327 * jnp.exp(-0.5 * inner * inner))
    grad_inner = (grad_active * slope).astype(BF16)
    own_inner = own_hidden(grad_inner)
    g_b_up = jnp.sum(own_inner, axis=0, dtype=F32)
    g_w_up = mm_tn(normed_low, own_inner)
    grad_normed = grad_second + mm(grad_inner, all_up)
    grad_first = norm_back(grad_normed, ln1_gain, hat1, rstd1)
    g_ln1_gain = jnp.sum(grad_normed * hat1, axis=0)
    g_ln1_bias = jnp.sum(grad_normed, axis=0)
    g_b_out = jnp.sum(grad_first, axis=0)
    first_low = grad_first.astype(BF16)
    g_w_out = mm_tn(own_part(att), first_low)
    grad_att = mm_nt(first_low, all_out).astype(BF16)
    dq, dk, dv = attend_back(lengths, q_picked, keys, values, grad_att.reshape(seqs, slots, width))
    dq_rows = dq.reshape(seqs * slots, width)
    dk_rows = dk.reshape(rows, width)
    dv_rows = dv.reshape(rows, width)
    own_q, own_k, own_v = own_part(dq_rows), own_part(dk_rows), own_part(dv_rows)
    g_b_qv = jnp.concatenate([jnp.sum(own_q, axis=0, dtype=F32), jnp.sum(own_v, axis=0, dtype=F32)])
    g_vectors = jnp.concatenate([
        g_b_out, g_ln1_gain, g_ln1_bias, g_b_down, g_ln2_gain, g_ln2_bias, g_b_up, g_b_qv,
        jnp.zeros((8 * width - 6 * width - hidden - 2 * part,), F32),
    ]).reshape(8, width)
    used_rows = part + 3 * part + 8
    g_last = jnp.concatenate([
        g_w_out, mm_tn(own_q, picked_rows), mm_tn(own_k, tokens), mm_tn(own_v, tokens), g_vectors,
        jnp.zeros((-used_rows % 128, width), F32),
    ], axis=0)
    g_w_down, g_w_up, g_last = dp_reduce(outer, [g_w_down, g_w_up, g_last], 384, 2)
    g_w_out, g_last = g_last[:part], g_last[part:]
    sparse = (grad_first + mm(dq_rows, all_qkv[0])).reshape(seqs, slots, width)
    grad_tokens = (
        jnp.einsum("spk,spd->skd", chosen_f32, sparse, precision=lax.Precision.HIGH,
                   preferred_element_type=F32).reshape(rows, width)
        + mm(dk_rows, all_qkv[1])
        + mm(dv_rows, all_qkv[2])
    )
    g_w_qkv = jnp.swapaxes(g_last[: 3 * part].reshape(3, part, width), 1, 2)
    g_vectors = g_last[3 * part :].reshape(-1)
    g_b_out, g_ln1_gain, g_ln1_bias, g_b_down, g_ln2_gain, g_ln2_bias = (
        g_vectors[i * width : (i + 1) * width] for i in range(6)
    )
    g_b_up = g_vectors[6 * width : 6 * width + hidden]
    g_b_qv = g_vectors[6 * width + hidden : 6 * width + hidden + 2 * part].reshape(2, part)
    return (
        output, grad_tokens, g_w_qkv, g_b_qv, g_w_out, g_b_out, g_ln1_gain, g_ln1_bias, g_w_up, g_b_up,
        g_w_down, g_b_down, g_ln2_gain, g_ln2_bias,
    )


def solution(mesh):
    in_specs = (
        P("dp", None), P(None, None, "tensor"), P(None, "tensor"), P("tensor", None), P(), P(), P(),
        P(None, "tensor"), P("tensor"), P("tensor", None), P(), P(), P(), P("dp"), P("dp", None), P("dp", None),
    )
    out_specs = (
        P("dp", None), P("dp", None), P(None, None, "tensor"), P(None, "tensor"), P("tensor", None), P(), P(),
        P(), P(None, "tensor"), P("tensor"), P("tensor", None), P(), P(), P(),
    )
    ranks, copies = mesh.shape["tensor"], mesh.shape["dp"]
    outer = None
    if copies > GROUP:
        outer = [[g + j for g in range(0, copies, GROUP)] for j in range(GROUP)]
    step = functools.partial(body, ranks, outer)
    return jax.shard_map(step, mesh=mesh, in_specs=in_specs, out_specs=out_specs, check_vma=False)
```

time: 537 us -> 409 us (0.76)
  the two profiles are of different devices: /device:TPU:0 before, /device:TPU:9 now
where the time goes in v2:
time: 409 us; the launch traced here: 403 us
  Pallas kernels  235 us (57%)
  matrix products  96.3 us (24%)
  local copies, waits for them, and re-layouts  45.7 us (11%)
  other arithmetic  23.9 us (6%)
    pallas_call x1, Pallas kernels, front(): pl.pallas_call(functools.partial(front_kernel, ranks, chunks), out_shape=...  132 us
    pallas_call x1, Pallas kernels, dp_reduce(): pl.pallas_call(functools.partial(reduce_kernel, tuple(chunks), len(arrays...  76 us
    dot_general x8, matrix products, mm(): return jnp.dot(a, b, preferred_element_type=F32)  41.4 us
    dot_general x4, matrix products, mm_nt(): lax.dot_general(a, b, (((1,), (1,)), ((), ())), preferred_element_type=F32)  30.2 us
    pallas_call x1, Pallas kernels, attend_back(): pl.pallas_call(attend_back_kernel, grid_spec=pltpu.PrefetchScalarGridSpec...  27.3 us
    unnamed x88, local copies, waits for them, and re-layouts  24.5 us
    dot_general x6, matrix products, mm_tn(): lax.dot_general(a, b, (((0,), (0,)), ((), ())), preferred_element_type=F32)  16.5 us
    another operation x1, other arithmetic  8.59 us

profile of v2, /device:TPU:9, one launch (start us, length us, event | category | flops | bytes accessed | tf_op | source)
XLA Modules:
  0.0 402.6 jit_solution(5582389835077248180)
XLA Ops:
  10.1 131.6 %front.1 = (bf16[4,512,768]{2,1,0:T(8,128)(2,1)}, bf16[4,512,768]{2,1,0:T(8,128)(2,1)}, bf16[4,128,768]{2,1,0:T(8,128)(2,1)}, bf16[4,512,768]{2,1,0:T(8,128)(2,1...) custom-call(bf16[4,512,768]{2,1,0:T(8,128)(2,1)} %bitcast.99, ...), custom_call_target="tpu_custom_call" | custom-call | tf_op jit(solution)/shard_map/front/pallas_call | solution.py:198
  141.7 8.6 %convert.6 = bf16[4,8,216,768]{3,2,1,0:T(8,128)(2,1)S(1)} convert(f32[4,8,216,768]{3,2,1,0:T(8,128)} %get-tuple-element.28) | non-fusion elementwise | flops 5308416 | bytes 31850496 | tf_op jit(solution)/shard_map/convert.3
  150.3 4.0 copy-done
  154.5 3.0 convolution_convert_fusion.1
  158.8 7.0 %fusion.64 = (bf16[4,8,96,768]{3,2,1,0:T(8,128)(2,1)}, bf16[4,8,96,768]{3,2,1,0:T(8,128)(2,1)S(1)}) fusion(bf16[4,8,216,768]{3,2,1,0:T(8,128)(2,1)} %copy-done), kind=kLoop, calls=%fused_computation.124 | loop fusion | bytes 18874368 | tf_op jit(solution)/shard_map/slice | solution.py:421
  167.9 5.5 %multiply_convert_fusion.2 = (bf16[512,3072]{1,0:T(8,128)(2,1)S(1)}, f32[512,3072]{1,0:T(8,128)S(1)}) fusion(f32[3072]{0:T(1024)S(1)} %bitcast.136, bf16[3072,768]{1,0:T(8,128)(2,1)} %bitcast.116, f32[512,768]{1,0:T(8,128)S(1)} %get-tuple-element.94, f32[768]{0:T(1024)S(1)} %copy-done.34, f32[768]{0:T(1024)S(1)} %copy-done.27, f32[512]{0:T(512)S(1)} %add_rsqrt_fusion.3, ...), kind=kOutput, calls=%fused_computation.11 | convolution fusion | flops 2427322368 | bytes 15751168 | tf_op jit(solution)/shard_map/dot_general | solution.py:275
  173.6 2.8 fusion.70
  182.1 4.7 %fusion.6 = bf16[512,3072]{1,0:T(8,128)(2,1)S(1)} fusion(f32[512,3072]{1,0:T(8,128)S(1)} %get-tuple-element.96, bf16[3072,768]{1,0:T(8,128)(2,1)S(1)} %bitcast.113, f32[3072]{0:T(1024)S(1)} %bitcast.137, f32[512,768]{1,0:T(8,128)S(1)} %get-tuple-element.84), kind=kOutput, calls=%fused_computation.8 | convolution fusion | flops 2433613824 | bytes 15740928 | tf_op jit(solution)/shard_map/dot_general | solution.py:275
  186.8 3.1 multiply_reduce_fusion.2
  193.4 27.3 %attend_back.1 = (bf16[4,128,768]{2,1,0:T(8,128)(2,1)}, bf16[4,512,768]{2,1,0:T(8,128)(2,1)}, bf16[4,512,768]{2,1,0:T(8,128)(2,1)}) custom-call(s32[4]{0:T(128)} %lengths_ref.3, bf16[4,128,768]{2,1,0:T(8,128)(2,1)} %get-tuple-element.30.q_ref, bf16[4,512,768]{2,1,0:T(8,128)(2,1)} %get-tuple-element.31.k_ref, bf16[4,512,768]{2,1,0:T(8,128)(2,1)} %get-tuple-element.32.v_ref, ...), custom_call_target="tpu_custom_call" | custom-call | flops 8053063680 | bytes 14155776 | tf_op jit(solution)/shard_map/attend_back/pallas_call | solution.py:234
  234.2 4.4 %fusion.37.refs_1_ = f32[768,768]{1,0:T(8,128)} fusion(bf16[512,3072]{1,0:T(8,128)(2,1)} %copy-done.22, s32[]{:T(128)S(6)} %select_n.30, f32[512,768]{1,0:T(8,128)S(1)} %copy-done.11, f32[768]{0:T(1024)S(1)} %copy-done.34, f32[768]{0:T(1024)S(1)} %copy-done.27, f32[512]{0:T(512)S(1)} %add_rsqrt_fusion.3, f32[512]{0:T(512)S(1)} %broadcast_multiply_fusion.6), kind=kOutput, calls=%fused_computation.70 | convolution fusion | flops 605945856 | bytes 4728836 | tf_op jit(solution)/shard_map/dot_general | solution.py:279
  238.6 3.4 fusion.35.refs_0_
  242.0 76.0 %dp_reduce.1 = (f32[768,768]{1,0:T(8,128)}, f32[768,768]{1,0:T(8,128)}, f32[896,768]{1,0:T(8,128)}) custom-call(f32[768,768]{1,0:T(8,128)} %fusion.35.refs_0_, f32[768,768]{1,0:T(8,128)} %fusion.37.refs_1_, f32[896,768]{1,0:T(8,128)} %copy-done.14), custom_call_target="tpu_custom_call" | custom-call | tf_op jit(solution)/shard_map/dp_reduce/pallas_call | solution.py:369
  318.0 2.8 slice.98
  327.7 2.8 convolution_add_fusion
  333.5 2.6 fusion.25
  336.1 5.2 %fusion.7 = f32[2048,768]{1,0:T(8,128)} fusion(f32[2048,768]{1,0:T(8,128)S(1)} %fusion.25, f32[4,512,768]{2,1,0:T(8,128)S(1)} %fusion.32, bf16[2048,768]{1,0:T(8,128)(2,1)S(1)} %bitcast.103, bf16[3,768,768]{2,1,0:T(8,128)(2,1)S(1)} %copy-done.16), kind=kOutput, calls=%fused_computation.10 | convolution fusion | flops 2419064832 | bytes 23199744 | tf_op jit(solution)/shard_map/dot_general | solution.py:271
  341.3 2.9 copy.37
  344.1 6.2 %fusion.65 = (f32[2048]{0:T(1024)S(1)}, f32[2048,768]{0,1:T(8,128)S(1)}) fusion(f32[768]{0:T(1024)S(1)} %copy-done.31, bf16[2048,768]{1,0:T(8,128)(2,1)} %bitcast.121, bf16[768,768]{1,0:T(8,128)(2,1)} %bitcast.132, bf16[2048,768]{0,1:T(8,128)(2,1)} %copy.37), kind=kOutput, calls=%fused_computation.125 | convolution fusion | flops 2422208512 | bytes 13773824 | tf_op jit(solution)/shard_map/dot_general | solution.py:271
  352.9 18.2 %multiply_convert_fusion.4.clone.4 = bf16[2048,3072]{1,0:T(8,128)(2,1)} fusion(f32[3072]{0:T(1024)S(1)} %bitcast.138, bf16[3072,768]{1,0:T(8,128)(2,1)} %bitcast.117, f32[2048,768]{0,1:T(8,128)S(1)} %get-tuple-element.90, f32[768]{0:T(1024)S(1)} %copy-done.35, f32[768]{0:T(1024)S(1)} %copy-done.27, ...), kind=kOutput, calls=%fused_computation.clone.clone.clone.clone.clone.clone.1 | convolution fusion | flops 9709289472 | bytes 23627776 | tf_op jit(solution)/shard_map/dot_general | solution.py:275
  371.1 17.9 %fusion.66 = (f32[2048]{0:T(1024)S(1)}, f32[2048,768]{0,1:T(8,128)}) fusion(f32[768]{0:T(1024)S(1)} %copy-done.33, bf16[3072,768]{1,0:T(8,128)(2,1)} %bitcast.114, f32[2048,768]{0,1:T(8,128)} %copy-done.7, f32[768]{0:T(1024)S(1)} %copy-done.35, f32[768]{0:T(1024)S(1)} %copy-done.27, f32[2048]{0:T(1024)S(1)} %add_rsqrt_fusion.1, ...), kind=kOutput, calls=%fused_computation.126 | convolution fusion | flops 9674684416 | bytes 29918208 | tf_op jit(solution)/shard_map/dot_general | solution.py:271
  389.0 3.6 multiply_reduce_fusion
  394.6 2.8 copy.42
  397.4 3.4 copy.57
  (141 shorter events, 51.1 us)
Async XLA Ops:
  0.6 6.8 %copy-start.30 = (f32[2,192]{1,0:T(2,128)S(1)}, f32[2,192]{1,0:T(2,128)}, u32[]{:S(2)}) copy-start(f32[2,192]{1,0:T(2,128)} %param.18) | copy-start | bytes 4612
  0.7 7.1 %copy-start.29 = (f32[768]{0:T(1024)S(1)}, f32[768]{0:T(1024)}, u32[]{:S(2)}) copy-start(f32[768]{0:T(1024)} %param.24) | copy-start | bytes 9220
  0.7 7.9 %copy-start.1 = (bf16[2048,768]{1,0:T(8,128)(2,1)S(1)}, bf16[2048,768]{1,0:T(8,128)(2,1)}, u32[]{:S(2)}) copy-start(bf16[2048,768]{1,0:T(8,128)(2,1)} %param.16) | copy-start | bytes 9437188
  0.7 7.8 %copy-start.24 = (s32[4,128]{1,0:T(4,128)S(1)}, s32[4,128]{1,0:T(4,128)}, u32[]{:S(2)}) copy-start(s32[4,128]{1,0:T(4,128)} %param.30) | copy-start | bytes 6148
  141.7 12.7 %copy-start.20 = (bf16[192,768]{1,0:T(8,128)(2,1)S(1)}, bf16[192,768]{1,0:T(8,128)(2,1)}, u32[]{:S(2)}) copy-start(bf16[192,768]{1,0:T(8,128)(2,1)} %param.19) | copy-start | bytes 884740
  154.5 36.1 %copy-start.19 = (bf16[4,192,768]{2,1,0:T(8,128)(2,1)}, bf16[4,192,768]{2,1,0:T(8,128)(2,1)S(1)}, u32[]{:S(2)}) copy-start(bf16[4,192,768]{2,1,0:T(8,128)(2,1)S(1)} %bitcast_dynamic-update-slice_fusion.2) | copy-start | bytes 3538948
  158.4 31.6 %copy-start.10 = (f32[512,768]{1,0:T(8,128)}, f32[512,768]{1,0:T(8,128)S(1)}, u32[]{:S(2)}) copy-start(f32[512,768]{1,0:T(8,128)S(1)} %get-tuple-element.94) | copy-start | bytes 4718596
  158.8 7.1 %copy-start.12 = (bf16[768,768]{0,1:T(8,128)(2,1)S(1)}, bf16[768,768]{0,1:T(8,128)(2,1)}, u32[]{:S(2)}) copy-start(bf16[768,768]{0,1:T(8,128)(2,1)} %copy.39) | copy-start | bytes 3538948
  158.8 9.1 %copy-start.27 = (f32[768]{0:T(1024)S(1)}, f32[768]{0:T(1024)}, u32[]{:S(2)}) copy-start(f32[768]{0:T(1024)} %param.21) | copy-start | bytes 9220
  158.8 9.1 %copy-start.34 = (f32[768]{0:T(1024)S(1)}, f32[768]{0:T(1024)}, u32[]{:S(2)}) copy-start(f32[768]{0:T(1024)} %param.22) | copy-start | bytes 9220
  167.9 14.2 %copy-start.25 = (f32[4,1,768]{2,1,0:T(1,128)}, f32[4,1,768]{2,1,0:T(1,128)S(1)}, u32[]{:S(2)}) copy-start(f32[4,1,768]{2,1,0:T(1,128)S(1)} %slice.93) | copy-start | bytes 36868
  167.9 5.6 %copy-start.17 = (bf16[768,768]{1,0:T(8,128)(2,1)S(1)}, bf16[768,768]{1,0:T(8,128)(2,1)}, u32[]{:S(2)}) copy-start(bf16[768,768]{1,0:T(8,128)(2,1)} %param.25) | copy-start | bytes 3538948
  167.9 5.7 %copy-start.32 = (f32[768]{0:T(1024)S(1)}, f32[768]{0:T(1024)}, u32[]{:S(2)}) copy-start(f32[768]{0:T(1024)} %param.26) | copy-start | bytes 9220
  173.6 8.5 %copy-start.13 = (bf16[4,768,768]{2,1,0:T(8,128)(2,1)}, bf16[4,768,768]{2,1,0:T(8,128)(2,1)S(1)}, u32[]{:S(2)}) copy-start(bf16[4,768,768]{2,1,0:T(8,128)(2,1)S(1)} %bitcast_dynamic-update-slice_fusion.1) | copy-start | bytes 14155780
  173.6 4.9 %slice-start = ((s8[6291456]{0:T(1024)(128)(4,1)}), s8[4194304]{0:T(1024)(128)(4,1)S(1)}, s32[]{:S(2)}) async-start(s8[6291456]{0:T(1024)(128)(4,1)} %bitcast.106), calls=%async_computation | async-start | bytes 8388608
  173.6 5.5 %slice-start.1 = ((s8[6291456]{0:T(1024)(128)(4,1)}), s8[2097152]{0:T(1024)(128)(4,1)S(1)}, s32[]{:S(2)}) async-start(s8[6291456]{0:T(1024)(128)(4,1)} %bitcast.106), calls=%async_computation.1 | async-start | bytes 4194304
  173.6 5.5 %copy-start.23 = (f32[768]{0:T(1024)S(1)}, f32[768]{0:T(1024)}, u32[]{:S(2)}) copy-start(f32[768]{0:T(1024)} %param.27) | copy-start | bytes 9220
  181.5 5.3 %slice-start.2 = ((s8[4718592]{0:T(1024)(128)(4,1)}), s8[4194304]{0:T(1024)(128)(4,1)S(1)}, s32[]{:S(2)}) async-start(s8[4718592]{0:T(1024)(128)(4,1)} %bitcast.118), calls=%async_computation.2 | async-start | bytes 8388608
  182.0 4.8 %copy-start.8 = (f32[512,768]{1,0:T(8,128)}, f32[512,768]{1,0:T(8,128)S(1)}, u32[]{:S(2)}) copy-start(f32[512,768]{1,0:T(8,128)S(1)} %get-tuple-element.84) | copy-start | bytes 4718596
  182.0 4.8 %slice-start.3 = ((s8[4718592]{0:T(1024)(128)(4,1)}), s8[524288]{0:T(1024)(128)(4,1)S(1)}, s32[]{:S(2)}) async-start(s8[4718592]{0:T(1024)(128)(4,1)} %bitcast.118), calls=%async_computation.3 | async-start | bytes 1048576
  220.6 8.4 %copy-start.2 = (bf16[2048,768]{1,0:T(8,128)(2,1)S(1)}, bf16[2048,768]{1,0:T(8,128)(2,1)}, u32[]{:S(2)}) copy-start(bf16[2048,768]{1,0:T(8,128)(2,1)} %param.16) | copy-start | bytes 9437188
  234.2 7.7 %copy-start.14 = (f32[896,768]{1,0:T(8,128)}, f32[896,768]{1,0:T(8,128)S(1)}, u32[]{:S(2)}) copy-start(f32[896,768]{1,0:T(8,128)S(1)} %broadcast_dynamic-update-slice_fusion.refs_2_) | copy-start | bytes 8257540
  352.9 18.2 %copy-start.33 = (f32[768]{0:T(1024)S(1)}, f32[768]{0:T(1024)}, u32[]{:S(2)}) copy-start(f32[768]{0:T(1024)} %param.26) | copy-start | bytes 9220
  389.0 4.6 %copy-start.28 = (f32[768]{0:T(1024)S(1)}, f32[768]{0:T(1024)}, u32[]{:S(2)}) copy-start(f32[768]{0:T(1024)} %param.28) | copy-start | bytes 9220
  (17 other events, 49.4 us)
